TPU v7x, 128 devices: a whole 4x4x4 slice. The times are simulated.
128 devices in a mesh: bond: 8 (over x, core), op: 16 (over y, z).
Axes of the slice: x: 4, y: 4, z: 4, core: 2. Of those that a mesh axis runs over, the one named last changes fastest.
Arguments:
- wave_slab: bfloat16 [8192, 8192], P('op', 'bond'), may hold values from -6 to 6
- left_blocks: bfloat16 [32, 16, 2, 128, 128], P('op'), may hold values from -0.375 to 0.375
- right_blocks: bfloat16 [32, 64, 2, 128, 128], P('op'), may hold values from -0.0625 to 0.0625
- sector_size: int32 [64], replicated, may hold values from 1 to 128
- left_pairs: int32 [32, 16, 2], P('op'), may hold values from 0 to 63
- right_pairs: int32 [32, 64, 2], P('op'), may hold values from 0 to 63
Outputs:
- applied: float32 [2048, 8192], P('bond', 'op')
All inputs are finite; a program needn't handle non-finite values.
Results may differ from a plain program's by a relative error of at most 0.0029.
Values may be sent and summed in bfloat16 or wider, within the bound.
No kernel may reach another device: no remote copies, remote signals or barrier semaphores. Data moves between devices by JAX's collectives and lax.ppermute only.
A program may use at most 128 MiB of HBM per device.

v0:
```python
import jax
import jax.numpy as jnp
from jax import lax
from jax.sharding import PartitionSpec as P

TILE = 128


def live_mask(sector_size):
    states = jnp.arange(TILE, dtype=jnp.int32)
    return (states[None, :] < sector_size[:, None]).astype(jnp.float32).reshape(-1)


def on_device(wave_slab, left_blocks, right_blocks, sector_size, left_pairs, right_pairs):
    live = live_mask(sector_size)
    local_rows = wave_slab.shape[0]
    strip = wave_slab.shape[1]
    row_live = lax.dynamic_slice_in_dim(live, lax.axis_index("op") * local_rows, local_rows)
    col_live = lax.dynamic_slice_in_dim(live, lax.axis_index("bond") * strip, strip)
    masked = (wave_slab.astype(jnp.float32) * row_live[:, None] * col_live[None, :]).astype(
        jnp.bfloat16
    )
    whole = lax.all_gather(masked, "op", axis=0, tiled=True)
    full_width = whole.shape[0]
    sector_count = full_width // TILE
    sectors = whole.reshape(sector_count, TILE, strip)
    term_count = left_blocks.shape[0]
    middles = []
    for term_idx in range(term_count):
        picked = sectors[left_pairs[term_idx]]
        middle = jnp.einsum(
            "ipxy,ipys->ixs", left_blocks[term_idx], picked, preferred_element_type=jnp.float32
        )
        middles.append(middle.astype(jnp.bfloat16).reshape(-1, strip))
    stacked = jnp.stack(middles, 0)
    bond_count = lax.axis_size("bond")
    slab_rows = stacked.shape[1]
    share_rows = slab_rows // bond_count
    blocked = stacked.reshape(term_count, bond_count, share_rows, strip)
    arrived = lax.all_to_all(blocked, "bond", split_axis=1, concat_axis=3, tiled=True)
    row_count = arrived.shape[2]
    total = jnp.zeros((row_count, sector_count, TILE), jnp.float32)
    for term_idx in range(term_count):
        split_cols = arrived[term_idx, 0].reshape(row_count, sector_count, TILE)
        chosen = split_cols[:, right_pairs[term_idx]]
        total = total + jnp.einsum(
            "rjpy,jpyz->rjz", chosen, right_blocks[term_idx], preferred_element_type=jnp.float32
        )
    partial_value = total.reshape(row_count, full_width)
    summed = lax.psum_scatter(partial_value, "op", scatter_dimension=1, tiled=True)
    out_cols = summed.shape[1]
    out_row_live = lax.dynamic_slice_in_dim(live, lax.axis_index("bond") * share_rows, share_rows)
    out_col_live = lax.dynamic_slice_in_dim(live, lax.axis_index("op") * out_cols, out_cols)
    return summed * out_row_live[:, None] * out_col_live[None, :]


def solution(mesh):
    placed = (
        P("op", "bond"),
        P("op", None, None, None, None),
        P("op", None, None, None, None),
        P(),
        P("op", None, None),
        P("op", None, None),
    )
    return jax.shard_map(
        on_device, mesh=mesh, in_specs=placed, out_specs=P("bond", "op"), check_vma=False
    )
```

profile of v0, /device:TPU:0, one launch (start us, length us, event | category | flops | bytes accessed | tf_op | source)
XLA Modules:
  0.0 447.6 jit_solution(14537597451842649991)
XLA Ops:
  6.5 0.7 convert_bitcast_fusion
  7.4 2.5 multiply_convert_fusion
  9.9 0.7 compare_select_fusion.3
  10.6 0.1 copy.25
  10.7 0.1 reshape.143
  10.9 0.1 reshape.151
  11.0 112.9 %all-gather.2.cloned.1.call-done = bf16[8192,1024]{1,0:T(8,128)(2,1)} async-done(((bf16[512,1024]{1,0:T(8,128)(2,1)}), bf16[8192,1024]{1,0:T(8,128)(2,1)}) %all-gather.2.cloned.1.call-update) | async-done | bytes 16777232 | tf_op jit(solution)/shard_map/all_gather | solution.py:23
  123.9 10.9 %gather_fusion = bf16[32,128,1024]{2,1,0:T(8,128)(2,1)} fusion(bf16[64,128,1024]{2,1,0:T(8,128)(2,1)} %bitcast.83, s32[1024]{0:T(1024)S(1)} %pad_clamp_fusion.3), kind=kCustom, calls=%fused_computation | custom fusion | bytes 16777344 | tf_op jit(solution)/shard_map/gather | solution.py:30
  134.8 6.6 %bitcast_convert_fusion.1 = bf16[16,1024,128]{1,2,0:T(8,128)(2,1)} fusion(bf16[16,2,128,1024]{3,2,1,0:T(8,128)(2,1)} %bitcast.76, bf16[2,16,2,128,128]{4,3,2,1,0:T(8,128)(2,1)S(1)} %copy-done), kind=kOutput, calls=%fused_computation.7 | convolution fusion | flops 1075838976 | bytes 13631488 | tf_op jit(solution)/shard_map/ipxy,ipys->ixs/dot_general | solution.py:31
  141.4 6.4 %copy.27 = bf16[1,8,256,1024]{2,3,0,1:T(8,128)(2,1)} copy(bf16[1,8,256,1024]{3,2,1,0:T(8,128)(2,1)} %bitcast.81) | data formatting | bytes 8388608 | tf_op jit(solution)/shard_map/stack | solution.py:35
  147.8 10.8 %gather_fusion.1 = bf16[32,128,1024]{2,1,0:T(8,128)(2,1)} fusion(bf16[64,128,1024]{2,1,0:T(8,128)(2,1)} %bitcast.84, s32[1024]{0:T(1024)S(1)} %pad_clamp_fusion.2), kind=kCustom, calls=%fused_computation.1 | custom fusion | bytes 16777344 | tf_op jit(solution)/shard_map/gather | solution.py:30
  158.6 6.6 %bitcast_convert_fusion = bf16[16,1024,128]{1,2,0:T(8,128)(2,1)} fusion(bf16[16,2,128,1024]{3,2,1,0:T(8,128)(2,1)} %bitcast.75, bf16[2,16,2,128,128]{4,3,2,1,0:T(8,128)(2,1)S(1)} %copy-done), kind=kOutput, calls=%fused_computation.6 | convolution fusion | flops 1075838976 | bytes 13631488 | tf_op jit(solution)/shard_map/ipxy,ipys->ixs/dot_general | solution.py:31
  165.2 6.5 %copy.28 = bf16[1,8,256,1024]{2,3,0,1:T(8,128)(2,1)} copy(bf16[1,8,256,1024]{3,2,1,0:T(8,128)(2,1)} %bitcast.82) | data formatting | bytes 8388608 | tf_op jit(solution)/shard_map/stack | solution.py:35
  171.7 7.5 %pad_maximum_fusion = bf16[2,8,256,1024]{2,3,0,1:T(8,128)(2,1)} fusion(bf16[1,8,256,1024]{2,3,0,1:T(8,128)(2,1)} %copy.28, bf16[1,8,256,1024]{2,3,0,1:T(8,128)(2,1)} %copy.27), kind=kLoop, calls=%fused_computation.4 | loop fusion | flops 4194304 | bytes 16777216 | tf_op jit(solution)/shard_map/stack | solution.py:35
  179.1 5.2 %all-to-all-start = ((bf16[2,8,256,1024]{2,3,0,1:T(8,128)(2,1)}), bf16[2,8,256,1024]{2,3,0,1:T(8,128)(2,1)}, u32[]{:S(2)}, u32[]{:S(2)}) async-start(bf16[2,8,256,1024]{2,3,0,1:T(8,128)(2,1)} %pad_maximum_fusion), calls=%async_computation | async-start | bytes 16777216 | tf_op jit(solution)/shard_map/all_to_all | solution.py:40
  184.3 0.2 reduce-scatter.2.cloned.1.call-start
  184.5 0.1 copy.33
  184.6 0.1 reshape.167
  184.8 0.1 copy.30
  184.9 0.1 reshape.159
  185.0 93.8 %all-to-all-done = bf16[2,8,256,1024]{2,3,0,1:T(8,128)(2,1)} async-done(((bf16[2,8,256,1024]{2,3,0,1:T(8,128)(2,1)}), bf16[2,8,256,1024]{2,3,0,1:T(8,128)(2,1)}, u32[]{:S(2)}, u32[]{:S(2)}) %all-to-all-start) | async-done | bytes 8388640 | tf_op jit(solution)/shard_map/all_to_all | solution.py:40
  278.9 7.3 %copy.44 = bf16[2,8,256,1024]{2,3,1,0:T(8,128)(2,1)} copy(bf16[2,8,256,1024]{2,3,0,1:T(8,128)(2,1)} %all-to-all-done) | data formatting | bytes 16777216 | tf_op jit(solution)/shard_map/all_to_all | solution.py:40
  286.2 5.7 %fusion.12 = (bf16[1,1,256,8,1024]{2,4,3,1,0:T(8,128)(2,1)}, bf16[1,1,256,8,1024]{2,4,3,1,0:T(8,128)(2,1)}) fusion(bf16[2,1,256,8,1024]{2,4,3,1,0:T(8,128)(2,1)} %bitcast.79), kind=kLoop, calls=%fused_computation.31 | loop fusion | bytes 16777216 | tf_op jit(solution)/shard_map/slice | solution.py:44
  291.9 6.4 %copy.34 = bf16[256,64,128]{2,0,1:T(8,128)(2,1)} copy(bf16[256,64,128]{0,2,1:T(8,128)(2,1)} %bitcast.86) | data formatting | bytes 8388608 | tf_op jit(solution)/shard_map/reshape;squeeze | solution.py:44
  298.3 6.3 %copy.31 = bf16[256,64,128]{2,0,1:T(8,128)(2,1)} copy(bf16[256,64,128]{0,2,1:T(8,128)(2,1)} %bitcast.85) | data formatting | bytes 8388608 | tf_op jit(solution)/shard_map/reshape;squeeze | solution.py:44
  304.6 8.8 %gather_fusion.3 = bf16[128,256,128]{2,1,0:T(8,128)(2,1)} fusion(bf16[256,64,128]{2,0,1:T(8,128)(2,1)} %copy.34, s32[1024]{0:T(1024)S(1)} %pad_clamp_fusion), kind=kCustom, calls=%fused_computation.3 | custom fusion | bytes 16777728 | tf_op jit(solution)/shard_map/gather | solution.py:45
  313.4 10.7 %fusion = f32[64,256,128,1]{1,2,3,0:T(8,128)} fusion(bf16[256,64,2,128]{3,0,2,1:T(8,128)(2,1)} %bitcast.80, bf16[2,64,2,128,128]{4,3,2,1,0:T(8,128)(2,1)} %param.8), kind=kOutput, calls=%fused_computation.9 | convolution fusion | flops 1073741824 | bytes 20971520 | tf_op jit(solution)/shard_map/rjpy,jpyz->rjz/dot_general | solution.py:46
  324.1 8.8 %gather_fusion.2 = bf16[128,256,128]{2,1,0:T(8,128)(2,1)} fusion(bf16[256,64,128]{2,0,1:T(8,128)(2,1)} %copy.31, s32[1024]{0:T(1024)S(1)} %pad_clamp_fusion.1), kind=kCustom, calls=%fused_computation.2 | custom fusion | bytes 16777728 | tf_op jit(solution)/shard_map/gather | solution.py:45
  332.8 13.2 %bitcast_add_fusion = f32[64,256,128]{1,2,0:T(8,128)} fusion(f32[64,256,128,1]{1,2,3,0:T(8,128)} %fusion, bf16[256,64,2,128]{3,0,2,1:T(8,128)(2,1)} %bitcast.77, bf16[2,64,2,128,128]{4,3,2,1,0:T(8,128)(2,1)} %param.8), kind=kOutput, calls=%fused_computation.5 | convolution fusion | flops 1075838976 | bytes 29360128 | tf_op jit(solution)/shard_map/rjpy,jpyz->rjz/dot_general | solution.py:46
  346.0 8.9 %copy.36 = f32[256,8192]{1,0:T(8,128)} copy(f32[256,8192]{0,1:T(8,128)} %bitcast.78) | data formatting | bytes 16777216 | tf_op jit(solution)/shard_map/reshape | solution.py:49
  355.0 83.9 %reduce-scatter.2.cloned.1.call-done = f32[256,512]{1,0:T(8,128)} async-done(((f32[256,8192]{1,0:T(8,128)}), f32[256,512]{1,0:T(8,128)}) %reduce-scatter.2.cloned.1.call-update) | async-done | bytes 524304 | tf_op jit(solution)/shard_map/reduce_scatter | solution.py:50
  438.9 1.9 multiply_multiply_fusion
  (16 shorter events, 0.3 us)
Async XLA Ops:
  6.5 117.3 %all-gather.2.cloned.1.call-start = ((), (), s32[]{:S(2)}) async-start(), calls=%async_computation.2 | async-start | bytes 17825792 | tf_op jit(solution)/shard_map/all_gather | solution.py:23
  123.9 10.9 %copy-start = (bf16[2,16,2,128,128]{4,3,2,1,0:T(8,128)(2,1)S(1)}, bf16[2,16,2,128,128]{4,3,2,1,0:T(8,128)(2,1)}, u32[]{:S(2)}) copy-start(bf16[2,16,2,128,128]{4,3,2,1,0:T(8,128)(2,1)} %param.7) | copy-start | bytes 6291460
  179.1 5.4 %copy-start.1 = (s32[2,64,2]{1,2,0:T(2,128)S(1)}, s32[2,64,2]{1,2,0:T(2,128)}, u32[]{:S(2)}) copy-start(s32[2,64,2]{1,2,0:T(2,128)} %param.11) | copy-start | bytes 3076
  179.1 99.8 %all-to-all-start = ((bf16[2,8,256,1024]{2,3,0,1:T(8,128)(2,1)}), bf16[2,8,256,1024]{2,3,0,1:T(8,128)(2,1)}, u32[]{:S(2)}, u32[]{:S(2)}) async-start(bf16[2,8,256,1024]{2,3,0,1:T(8,128)(2,1)} %pad_maximum_fusion), calls=%async_computation | async-start | bytes 16777216 | tf_op jit(solution)/shard_map/all_to_all | solution.py:40
  184.3 254.6 %reduce-scatter.2.cloned.1.call-start = ((), (), s32[]{:S(2)}) async-start(), calls=%async_computation.3 | async-start | bytes 8912896 | tf_op jit(solution)/shard_map/reduce_scatter | solution.py:50
Sparse Core Ops, SparseCore 0:
  10.0 113.8 all-gather.1
  355.0 83.7 reduce-scatter.1
where the time goes:
time: 449 us; the launch traced here: 448 us
  waiting for transfers between devices  291 us (65%)
  local copies, waits for them, and re-layouts  87.8 us (20%)
  matrix products  37 us (8%)
  between operations  13.5 us (3%)
  other arithmetic  13.4 us (3%)
  starting transfers between devices  5.4 us (1%)
    all_gather x1, waiting for transfers between devices, on_device(): whole = lax.all_gather(masked, 'op', axis=0, tiled=True)  113 us
    all_to_all x1, waiting for transfers between devices, on_device(): lax.all_to_all(blocked, 'bond', split_axis=1, concat_axis=3, tiled=True)  93.8 us
    reduce_scatter x1, waiting for transfers between devices, on_device(): lax.psum_scatter(partial_value, 'op', scatter_dimension=1, tiled=True)  83.9 us
    dot_general x2, matrix products, on_device(): jnp.einsum('rjpy,jpyz->rjz', chosen, right_blocks[term_idx], preferred_el...  23.8 us
    gather x2, local copies, waits for them, and re-layouts, on_device(): picked = sectors[left_pairs[term_idx]]  21.7 us
    gather x2, local copies, waits for them, and re-layouts, on_device(): chosen = split_cols[:, right_pairs[term_idx]]  17.6 us
    dot_general x2, matrix products, on_device(): jnp.einsum('ipxy,ipys->ixs', left_blocks[term_idx], picked, preferred_ele...  13.2 us
    another operation x2, local copies, waits for them, and re-layouts, on_device(): stacked = jnp.stack(middles, 0)  12.9 us
  transfers between devices with their start and end apart: 3, of which 3 were waited for; matrix products, arithmetic and copies ran while one was open for 0% of the time, Pallas kernels for 0%

commit v1 on v0

--- a/solution.py
+++ b/solution.py
@@ -37,7 +37,9 @@
     slab_rows = stacked.shape[1]
     share_rows = slab_rows // bond_count
     blocked = stacked.reshape(term_count, bond_count, share_rows, strip)
-    arrived = lax.all_to_all(blocked, "bond", split_axis=1, concat_axis=3, tiled=True)
+    pieces = jnp.split(blocked, lax.axis_size("bond"), axis=1)
+    received = lax.all_to_all(jnp.stack(pieces), "bond", 0, 0)
+    arrived = jnp.concatenate(received, axis=3)
     row_count = arrived.shape[2]
     total = jnp.zeros((row_count, sector_count, TILE), jnp.float32)
     for term_idx in range(term_count):

time: 449 us -> 453 us (level)
    unnamed x0 -> x7, other arithmetic: none -> 8.75 us
    another operation x1, other arithmetic: 7.46 us -> 1.08 us  [on_device(): received = lax.all_to_all(jnp.stack(pieces), 'bond', 0, 0)]
where the time goes in v1:
time: 453 us; the launch traced here: 452 us
  waiting for transfers between devices  290 us (64%)
  local copies, waits for them, and re-layouts  89.7 us (20%)
  matrix products  37 us (8%)
  other arithmetic  15.7 us (3%)
  between operations  13.5 us (3%)
  starting transfers between devices  5.38 us (1%)
    all_gather x1, waiting for transfers between devices, on_device(): whole = lax.all_gather(masked, 'op', axis=0, tiled=True)  113 us
    all_to_all x1, waiting for transfers between devices, on_device(): received = lax.all_to_all(jnp.stack(pieces), 'bond', 0, 0)  93.8 us
    reduce_scatter x1, waiting for transfers between devices, on_device(): lax.psum_scatter(partial_value, 'op', scatter_dimension=1, tiled=True)  83.7 us
    dot_general x2, matrix products, on_device(): jnp.einsum('rjpy,jpyz->rjz', chosen, right_blocks[term_idx], preferred_el...  23.8 us
    gather x2, local copies, waits for them, and re-layouts, on_device(): picked = sectors[left_pairs[term_idx]]  21.8 us
    gather x2, local copies, waits for them, and re-layouts, on_device(): chosen = split_cols[:, right_pairs[term_idx]]  17.5 us
    dot_general x2, matrix products, on_device(): jnp.einsum('ipxy,ipys->ixs', left_blocks[term_idx], picked, preferred_ele...  13.2 us
    another operation x2, local copies, waits for them, and re-layouts, on_device(): stacked = jnp.stack(middles, 0)  12.9 us
  transfers between devices with their start and end apart: 3, of which 3 were waited for; matrix products, arithmetic and copies ran while one was open for 0% of the time, Pallas kernels for 0%

profile of v1, /device:TPU:0, one launch (start us, length us, event | category | flops | bytes accessed | tf_op | source)
XLA Modules:
  0.0 451.8 jit_solution(15249644536887594395)
XLA Ops:
  6.5 0.7 convert_bitcast_fusion
  7.4 2.5 multiply_convert_fusion
  9.9 0.7 compare_select_fusion.3
  11.0 112.9 %all-gather.2.cloned.1.call-done = bf16[8192,1024]{1,0:T(8,128)(2,1)} async-done(((bf16[512,1024]{1,0:T(8,128)(2,1)}), bf16[8192,1024]{1,0:T(8,128)(2,1)}) %all-gather.2.cloned.1.call-update) | async-done | bytes 16777232 | tf_op jit(solution)/shard_map/all_gather | solution.py:23
  123.9 11.0 %gather_fusion = bf16[32,128,1024]{2,1,0:T(8,128)(2,1)} fusion(bf16[64,128,1024]{2,1,0:T(8,128)(2,1)} %bitcast.113, s32[1024]{0:T(1024)S(1)} %get-tuple-element.14), kind=kCustom, calls=%fused_computation | custom fusion | bytes 16777344 | tf_op jit(solution)/shard_map/gather | solution.py:30
  134.9 6.6 %bitcast_convert_fusion.1 = bf16[16,1024,128]{1,2,0:T(8,128)(2,1)} fusion(bf16[16,2,128,1024]{3,2,1,0:T(8,128)(2,1)} %bitcast.106, bf16[2,16,2,128,128]{4,3,2,1,0:T(8,128)(2,1)S(1)} %copy-done.2), kind=kOutput, calls=%fused_computation.20 | convolution fusion | flops 1075838976 | bytes 13631488 | tf_op jit(solution)/shard_map/ipxy,ipys->ixs/dot_general | solution.py:31
  141.5 6.5 %copy.41 = bf16[1,8,256,1024]{2,3,0,1:T(8,128)(2,1)} copy(bf16[1,8,256,1024]{3,2,1,0:T(8,128)(2,1)} %bitcast.111) | data formatting | bytes 8388608 | tf_op jit(solution)/shard_map/stack | solution.py:35
  148.0 10.8 %gather_fusion.1 = bf16[32,128,1024]{2,1,0:T(8,128)(2,1)} fusion(bf16[64,128,1024]{2,1,0:T(8,128)(2,1)} %bitcast.114, s32[1024]{0:T(1024)S(1)} %get-tuple-element.13), kind=kCustom, calls=%fused_computation.1 | custom fusion | bytes 16777344 | tf_op jit(solution)/shard_map/gather | solution.py:30
  158.7 6.6 %bitcast_convert_fusion = bf16[16,1024,128]{1,2,0:T(8,128)(2,1)} fusion(bf16[16,2,128,1024]{3,2,1,0:T(8,128)(2,1)} %bitcast.105, bf16[2,16,2,128,128]{4,3,2,1,0:T(8,128)(2,1)S(1)} %copy-done.2), kind=kOutput, calls=%fused_computation.19 | convolution fusion | flops 1075838976 | bytes 13631488 | tf_op jit(solution)/shard_map/ipxy,ipys->ixs/dot_general | solution.py:31
  165.3 6.4 %copy.42 = bf16[1,8,256,1024]{2,3,0,1:T(8,128)(2,1)} copy(bf16[1,8,256,1024]{3,2,1,0:T(8,128)(2,1)} %bitcast.112) | data formatting | bytes 8388608 | tf_op jit(solution)/shard_map/stack | solution.py:35
  171.8 2.4 bitcast_dynamic-update-slice_fusion.6
  174.6 1.3 copy-done.1
  175.9 1.1 bitcast_dynamic-update-slice_fusion.5
  177.0 1.0 bitcast_dynamic-update-slice_fusion.4
  178.0 1.1 bitcast_dynamic-update-slice_fusion.3
  179.1 1.0 bitcast_dynamic-update-slice_fusion.2
  180.1 1.1 bitcast_dynamic-update-slice_fusion.1
  181.2 1.1 bitcast_dynamic-update-slice_fusion
  182.3 1.1 fusion.16
  183.4 5.2 %all-to-all-start = ((bf16[8,2,1,256,1024]{3,4,2,1,0:T(8,128)(2,1)}), bf16[8,2,1,256,1024]{3,4,2,1,0:T(8,128)(2,1)}, u32[]{:S(2)}, u32[]{:S(2)}) async-start(bf16[8,2,1,256,1024]{3,4,2,1,0:T(8,128)(2,1)} %fusion.16), calls=%async_computation | async-start | bytes 16777216 | tf_op jit(solution)/shard_map/all_to_all | solution.py:41
  189.3 93.8 %all-to-all-done = bf16[8,2,1,256,1024]{3,4,2,1,0:T(8,128)(2,1)} async-done(((bf16[8,2,1,256,1024]{3,4,2,1,0:T(8,128)(2,1)}), bf16[8,2,1,256,1024]{3,4,2,1,0:T(8,128)(2,1)}, u32[]{:S(2)}, u32[]{:S(2)}) %all-to-all-start) | async-done | bytes 8388640 | tf_op jit(solution)/shard_map/all_to_all | solution.py:41
  283.1 7.4 %copy.65 = bf16[8,2,1,256,1024]{3,4,0,2,1:T(8,128)(2,1)} copy(bf16[8,2,1,256,1024]{3,4,2,1,0:T(8,128)(2,1)} %all-to-all-done) | data formatting | bytes 16777216 | tf_op jit(solution)/shard_map/all_to_all | solution.py:41
  290.5 5.7 %fusion.21 = (bf16[1,1,256,8,1024]{2,4,3,1,0:T(8,128)(2,1)}, bf16[1,1,256,8,1024]{2,4,3,1,0:T(8,128)(2,1)}) fusion(bf16[2,1,256,8,1024]{2,4,3,1,0:T(8,128)(2,1)} %bitcast.109), kind=kLoop, calls=%fused_computation.61 | loop fusion | bytes 16777216 | tf_op jit(solution)/shard_map/slice | solution.py:46
  296.2 6.4 %copy.55 = bf16[256,64,128]{2,0,1:T(8,128)(2,1)} copy(bf16[256,64,128]{0,2,1:T(8,128)(2,1)} %bitcast.116) | data formatting | bytes 8388608 | tf_op jit(solution)/shard_map/reshape;squeeze | solution.py:46
  302.7 6.4 %copy.52 = bf16[256,64,128]{2,0,1:T(8,128)(2,1)} copy(bf16[256,64,128]{0,2,1:T(8,128)(2,1)} %bitcast.115) | data formatting | bytes 8388608 | tf_op jit(solution)/shard_map/reshape;squeeze | solution.py:46
  309.0 8.7 %gather_fusion.3 = bf16[128,256,128]{2,1,0:T(8,128)(2,1)} fusion(bf16[256,64,128]{2,0,1:T(8,128)(2,1)} %copy.55, s32[1024]{0:T(1024)S(1)} %get-tuple-element.11), kind=kCustom, calls=%fused_computation.3 | custom fusion | bytes 16777728 | tf_op jit(solution)/shard_map/gather | solution.py:47
  317.8 10.7 %fusion = f32[64,256,128,1]{1,2,3,0:T(8,128)} fusion(bf16[256,64,2,128]{3,0,2,1:T(8,128)(2,1)} %bitcast.110, bf16[2,64,2,128,128]{4,3,2,1,0:T(8,128)(2,1)} %param.8), kind=kOutput, calls=%fused_computation.22 | convolution fusion | flops 1073741824 | bytes 20971520 | tf_op jit(solution)/shard_map/rjpy,jpyz->rjz/dot_general | solution.py:48
  328.4 8.7 %gather_fusion.2 = bf16[128,256,128]{2,1,0:T(8,128)(2,1)} fusion(bf16[256,64,128]{2,0,1:T(8,128)(2,1)} %copy.52, s32[1024]{0:T(1024)S(1)} %get-tuple-element.12), kind=kCustom, calls=%fused_computation.2 | custom fusion | bytes 16777728 | tf_op jit(solution)/shard_map/gather | solution.py:47
  337.2 13.2 %bitcast_add_fusion = f32[64,256,128]{1,2,0:T(8,128)} fusion(f32[64,256,128,1]{1,2,3,0:T(8,128)} %fusion, bf16[256,64,2,128]{3,0,2,1:T(8,128)(2,1)} %bitcast.107, bf16[2,64,2,128,128]{4,3,2,1,0:T(8,128)(2,1)} %param.8), kind=kOutput, calls=%fused_computation.18 | convolution fusion | flops 1075838976 | bytes 29360128 | tf_op jit(solution)/shard_map/rjpy,jpyz->rjz/dot_general | solution.py:48
  350.3 8.9 %copy.57 = f32[256,8192]{1,0:T(8,128)} copy(f32[256,8192]{0,1:T(8,128)} %bitcast.108) | data formatting | bytes 16777216 | tf_op jit(solution)/shard_map/reshape | solution.py:51
  359.3 83.7 %reduce-scatter.2.cloned.1.call-done = f32[256,512]{1,0:T(8,128)} async-done(((f32[256,8192]{1,0:T(8,128)}), f32[256,512]{1,0:T(8,128)}) %reduce-scatter.2.cloned.1.call-update) | async-done | bytes 524304 | tf_op jit(solution)/shard_map/reduce_scatter | solution.py:52
  443.0 1.9 multiply_multiply_fusion
  (25 shorter events, 1.7 us)
Async XLA Ops:
  6.5 117.3 %all-gather.2.cloned.1.call-start = ((), (), s32[]{:S(2)}) async-start(), calls=%async_computation.2 | async-start | bytes 17825792 | tf_op jit(solution)/shard_map/all_gather | solution.py:23
  123.9 11.0 %copy-start.2 = (bf16[2,16,2,128,128]{4,3,2,1,0:T(8,128)(2,1)S(1)}, bf16[2,16,2,128,128]{4,3,2,1,0:T(8,128)(2,1)}, u32[]{:S(2)}) copy-start(bf16[2,16,2,128,128]{4,3,2,1,0:T(8,128)(2,1)} %param.7) | copy-start | bytes 6291460
  171.8 2.9 copy-start
  171.8 4.2 copy-start.1
  183.4 5.4 %copy-start.3 = (s32[2,64,2]{1,2,0:T(2,128)S(1)}, s32[2,64,2]{1,2,0:T(2,128)}, u32[]{:S(2)}) copy-start(s32[2,64,2]{1,2,0:T(2,128)} %param.11) | copy-start | bytes 3076
  183.4 99.7 %all-to-all-start = ((bf16[8,2,1,256,1024]{3,4,2,1,0:T(8,128)(2,1)}), bf16[8,2,1,256,1024]{3,4,2,1,0:T(8,128)(2,1)}, u32[]{:S(2)}, u32[]{:S(2)}) async-start(bf16[8,2,1,256,1024]{3,4,2,1,0:T(8,128)(2,1)} %fusion.16), calls=%async_computation | async-start | bytes 16777216 | tf_op jit(solution)/shard_map/all_to_all | solution.py:41
  188.5 254.5 %reduce-scatter.2.cloned.1.call-start = ((), (), s32[]{:S(2)}) async-start(), calls=%async_computation.3 | async-start | bytes 8912896 | tf_op jit(solution)/shard_map/reduce_scatter | solution.py:52
Sparse Core Ops, SparseCore 0:
  10.0 113.8 all-gather.1
  359.4 83.6 reduce-scatter.1
